TPU v7x, 512 devices: a whole 4x4x16 slice. The times are simulated.
512 devices in a mesh: ex: 128 (over y, x, z_lo), tok: 4 (over z_hi, core).
Axes of the slice: x: 4, y: 4, z: 16 (z_hi: 2, z_lo: 8; z = z_hi * 8 + z_lo), core: 2. Of those that a mesh axis runs over, the one named last changes fastest.
Arguments:
- proj_rows: bfloat16 [1048576, 128], P(('ex', 'tok')), may hold values from -6 to 6
- query_features: bfloat16 [8192, 4096], P('ex'), may hold values from -0.09375 to 0.09375
- doc_lengths: int32 [128, 32], P('ex'), may hold values from 1 to 4096, 8192 in all within a row
- owner_map: int32 [128, 32], P('ex'), may hold values from 0 to 31, each once within a row
Outputs:
- scores: float32 [8192, 4096], P('ex', 'tok')
Inputs may be any that keep to these rules, and one draw needn't show every extreme that they name: `owner_map`: each row lists the slots 0 to 31 once each. `doc_lengths`: each row sums to 8192; its largest entry is exactly 4096.
All inputs are finite; a program needn't handle non-finite values.
Results may differ from a plain program's by a relative error of at most 0.0029.
Values may be sent and summed in bfloat16 or wider, within the bound.
A program may use at most 64 MiB of HBM per device.

v0:
```python
import jax
import jax.numpy as jnp
from jax import lax
from jax.sharding import PartitionSpec as P


def slot_lookup(lengths, owner_slots, positions):
    doc_ends = jnp.cumsum(lengths)
    doc_index = jnp.sum((positions[:, None] >= doc_ends[None, :]).astype(jnp.int32), axis=1)
    doc_match = doc_index[:, None] == jnp.arange(lengths.shape[0], dtype=jnp.int32)[None, :]
    return jnp.sum(jnp.where(doc_match, owner_slots[None, :], 0), axis=1)


def kron_sums(row_data, slots, targets):
    proj_width = row_data.shape[1] // 2
    count = row_data.shape[0]
    input_rows = row_data[:, :proj_width]
    grad_rows = row_data[:, proj_width:]

    def slot_group(slot_set):
        slot_mask = (slots[:, None] == slot_set[None, :]).astype(jnp.bfloat16)
        spread = (slot_mask[:, :, None] * grad_rows[:, None, :]).reshape(count, 4 * proj_width)
        return jnp.einsum("ta,tb->ab", spread, input_rows, preferred_element_type=jnp.float32)

    result = lax.map(slot_group, targets.reshape(-1, 4))
    return result.reshape(targets.shape[0], proj_width * proj_width)


def body(proj_rows, query_features, doc_lengths, owner_map):
    lengths = doc_lengths[0]
    owner_slots = owner_map[0]
    tok_count = lax.axis_size("tok")
    doc_dev = owner_slots.shape[0] // tok_count
    tok_index = lax.axis_index("tok")
    targets = tok_index * doc_dev + jnp.arange(doc_dev, dtype=jnp.int32)
    portion = lax.all_gather(proj_rows, "tok", axis=0, tiled=True)
    positions = jnp.arange(portion.shape[0], dtype=jnp.int32)
    summed = kron_sums(portion, slot_lookup(lengths, owner_slots, positions), targets)
    own_lengths = jnp.sum(
        jnp.where(owner_slots[None, :] == targets[:, None], lengths[None, :], 0), axis=1
    )
    features = (summed / jnp.sqrt(own_lengths.astype(jnp.float32))[:, None]).astype(jnp.bfloat16)
    return jnp.einsum(
        "qf,df->qd",
        query_features,
        lax.all_gather(features, "ex", axis=0, tiled=True),
        preferred_element_type=jnp.float32,
    )


def solution(mesh):
    placed = (P(("ex", "tok"), None), P("ex", None), P("ex", None), P("ex", None))
    return jax.shard_map(
        body, mesh=mesh, in_specs=placed, out_specs=P("ex", "tok"), check_vma=False
    )
```

profile of v0, /device:TPU:0, one launch (start us, length us, event | category | flops | bytes accessed | tf_op | source)
XLA Modules:
  0.0 1094.7 jit_solution(13539632485198462072)
XLA Ops:
  6.5 0.7 all-gather.3.cloned.1.call-update
  7.3 0.0 all-gather.5.cloned.1.call-start
  7.3 0.7 copy.9
  8.1 0.1 reduce-window.8
  8.1 0.1 reduce
  8.3 0.9 select_reduce_fusion.1
  9.1 0.2 convert_reduce_fusion
  9.3 0.9 select_reduce_fusion
  10.3 74.3 %all-gather.3.cloned.1.call-done = bf16[8192,128]{1,0:T(8,128)(2,1)} async-done(((bf16[2048,128]{1,0:T(8,128)(2,1)}), bf16[8192,128]{1,0:T(8,128)(2,1)}) %all-gather.3.cloned.1.call-update) | async-done | bytes 2097168 | tf_op jit(solution)/shard_map/all_gather | solution.py:36
  84.5 4.3 fusion.2
  88.8 2.7 copy.10
  91.5 6.2 while.10
  91.5 0.1 compare_convert_fusion.2
  91.6 1.6 broadcast_multiply_fusion.2
  93.2 1.4 fusion.14
  94.6 0.1 compare_convert_fusion.2
  94.7 1.6 broadcast_multiply_fusion.2
  96.3 1.4 fusion.14
  97.7 0.1 copy.11
  97.9 0.1 reshape.75
  98.0 0.7 divide_convert_fusion
  98.7 0.0 all-gather.5.cloned.1.call-update
  98.7 982.3 %all-gather.5.cloned.1.call-done = bf16[1024,4096]{1,0:T(8,128)(2,1)} async-done(((bf16[8,4096]{1,0:T(8,128)(2,1)}), bf16[1024,4096]{1,0:T(8,128)(2,1)}) %all-gather.5.cloned.1.call-update) | async-done | bytes 8388624 | tf_op jit(solution)/shard_map/all_gather | solution.py:46
  1081.1 6.7 convolution_bitcast_fusion.1
  (9 shorter events, 0.0 us)
Async XLA Ops:
  6.5 1074.5 %copy-start = (bf16[64,4096]{1,0:T(8,128)(2,1)S(1)}, bf16[64,4096]{1,0:T(8,128)(2,1)}, u32[]{:S(2)}) copy-start(bf16[64,4096]{1,0:T(8,128)(2,1)} %param.7) | copy-start | bytes 1572868
  6.5 78.0 %all-gather.3.cloned.1.call-start = ((), (), s32[]{:S(2)}) async-start(), calls=%async_computation | async-start | bytes 2621440 | tf_op jit(solution)/shard_map/all_gather | solution.py:36
  7.3 1073.8 %all-gather.5.cloned.1.call-start = ((), (), s32[]{:S(2)}) async-start(), calls=%async_computation.1 | async-start | bytes 8454144 | tf_op jit(solution)/shard_map/all_gather | solution.py:46
Sparse Core Ops, SparseCore 0:
  9.5 75.0 all-gather.2
  98.9 982.1 all-gather.4
where the time goes:
time: 1090 us
  waiting for transfers between devices  1060 us (97%)
  between operations  13.5 us (1%)
    all_gather x1, waiting for transfers between devices, body(): lax.all_gather(features, 'ex', axis=0, tiled=True)  982 us
    all_gather x1, waiting for transfers between devices, body(): portion = lax.all_gather(proj_rows, 'tok', axis=0, tiled=True)  74.3 us
  transfers between devices with their start and end apart: 2, of which 2 were waited for; matrix products, arithmetic and copies ran while one was open for 0% of the time, Pallas kernels for 0%

commit v1 on v0

v1 whole, which is shorter than its diff:
```python
import jax
import jax.numpy as jnp
from jax import lax
from jax.experimental import pallas as pl
from jax.experimental.pallas import tpu as pltpu
from jax.sharding import PartitionSpec as P

MESH = pl.DeviceIdType.MESH
F32 = jnp.float32
BF16 = jnp.bfloat16


def kernel(
    rows_ref, lens_ref, owner_ref, q_hbm, out_ref,
    xx, gt, mask, part, sib_recv, dsend, drecv, dall, qa, qb, sc_a, sc_b, pk, pk_recv, fin, fin_recv,
    sib_s, sib_r, q1_s, q1_r, q2_s, q2_r, ql, pi_s, pi_r, sw_s, sw_r, qd_s, qd_r, s2_s, s2_r, o_s, o_r,
):
    ex, tok = lax.axis_index("ex"), lax.axis_index("tok")
    y, x, p = ex // 32, lax.rem(ex // 8, 4), lax.rem(ex, 8)
    h, c = tok // 2, lax.rem(tok, 2)
    b, k = p // 4, lax.rem(p, 4)

    def at(yy, xx_, pp, hh, cc):
        return {"ex": (yy * 4 + xx_) * 8 + pp, "tok": hh * 2 + cc}

    def plane(dy, dx):
        return at(lax.rem(y + dy, 4), lax.rem(x + dx, 4), p, h, c)

    far = lax.rem(p + 4, 8)
    sibling = at(y, x, p, h, 1 - c)
    near_far = at(y, x, far, h, c)
    other_far = at(y, x, far, 1 - h, c)

    def quad(d):
        return at(y, x, b * 4 + lax.rem(k + d, 4), h, c)

    offsets = [(dy, dx) for dy in range(4) for dx in range(4) if dy or dx]
    partners = [plane(*o) for o in offsets] + [quad(d) for d in (1, 2, 3)] + [sibling, near_far, other_far]

    barrier = pltpu.get_barrier_semaphore()
    for partner in partners:
        pl.semaphore_signal(barrier, inc=1, device_id=partner, device_id_type=MESH)

    lens = lens_ref[...].astype(F32)
    owner = owner_ref[...]
    lane = lax.broadcasted_iota(jnp.int32, (32, 32), 1)
    slot = lax.broadcasted_iota(jnp.int32, (32, 32), 0)
    match = jnp.broadcast_to(owner, (32, 32)) == slot
    lens_b = jnp.broadcast_to(lens, (32, 32))
    order = jnp.sum(jnp.where(match, lane.astype(F32), 0.0), axis=1, keepdims=True)
    size = jnp.sum(jnp.where(match, lens_b, 0.0), axis=1, keepdims=True)
    begin = jnp.sum(jnp.where(lane.astype(F32) < order, lens_b, 0.0), axis=1, keepdims=True)
    end = begin + size
    scale = 1.0 / jnp.sqrt(size)
    pos = (lax.broadcasted_iota(jnp.int32, (32, 2048), 1) + tok * 2048).astype(F32)
    mask[...] = jnp.where((pos >= begin) & (pos < end), 1.0, 0.0)

    pick_r = lax.broadcasted_iota(jnp.int32, (64, 128), 0)
    pick_c = lax.broadcasted_iota(jnp.int32, (64, 128), 1)
    pick_g = (pick_c == pick_r + 64).astype(BF16)
    gt[...] = lax.dot_general(pick_g, rows_ref[...], (((1,), (1,)), ((), ())), preferred_element_type=F32)
    twice_r = lax.broadcasted_iota(jnp.int32, (128, 128), 0)
    twice_c = lax.broadcasted_iota(jnp.int32, (128, 128), 1)
    twice = ((twice_r == twice_c) | (twice_r + 64 == twice_c)).astype(F32)
    twice = jnp.where(twice_r < 64, twice, 0.0).astype(BF16)
    xx[...] = jnp.dot(rows_ref[...], twice, preferred_element_type=F32).astype(BF16)

    low = lax.broadcasted_iota(jnp.int32, (32, 128), 1) < 64

    def kron_half(half, dest):
        def step(n, carry):
            blocks = []
            for i in range(16):
                g_row = gt[pl.ds(half * 32 + n * 16 + i, 1), :]
                blocks.append((mask[...] * g_row).astype(BF16))
            spread = jnp.concatenate(blocks, axis=0)
            res = jnp.dot(spread, xx[...], preferred_element_type=F32)
            for i in range(8):
                even = res[64 * i:64 * i + 32]
                odd = res[64 * i + 32:64 * i + 64]
                dest[:, pl.ds(pl.multiple_of((n * 8 + i) * 128, 128), 128)] = jnp.where(low, even, odd)
            return carry

        lax.fori_loop(0, 2, step, 0)

    kron_half(1 - c, part.at[0])
    pl.semaphore_wait(barrier, len(partners))

    def send(src, dst, ss, rs, to):
        cp = pltpu.make_async_remote_copy(
            src_ref=src, dst_ref=dst, send_sem=ss, recv_sem=rs, device_id=to, device_id_type=MESH
        )
        cp.start()
        return cp

    sib = send(part.at[0], sib_recv, sib_s, sib_r, sibling)

    cols_a = pl.ds(pl.multiple_of(c * 2048, 1024), 1024)
    cols_b = pl.ds(pl.multiple_of(c * 2048 + 1024, 1024), 1024)
    q1 = []
    for n, d in enumerate((1, 2, 3)):
        q1.append(send(q_hbm.at[:, cols_a], qa.at[y, x], q1_s.at[n], q1_r.at[n], plane(0, d)))
        q1.append(send(q_hbm.at[:, cols_b], qb.at[x, y], q1_s.at[n + 3], q1_r.at[n + 3], plane(d, 0)))
    own_a = pltpu.make_async_copy(q_hbm.at[:, cols_a], qa.at[y, x], ql.at[0])
    own_b = pltpu.make_async_copy(q_hbm.at[:, cols_b], qb.at[x, y], ql.at[1])
    own_a.start()
    own_b.start()

    kron_half(c, part.at[1])
    sib.wait_recv()
    feats = ((part[1] + sib_recv[...]) * scale).astype(BF16)
    dsend[0] = feats[:16]
    dsend[1] = feats[16:]
    pi = [
        send(dsend.at[h], drecv.at[0], pi_s.at[0], pi_r.at[0], near_far),
        send(dsend.at[1 - h], drecv.at[1], pi_s.at[1], pi_r.at[1], other_far),
    ]

    own_a.wait()
    own_b.wait()
    for cp in q1:
        cp.wait()
    q2 = []
    for n, d in enumerate((1, 2, 3)):
        q2.append(send(qa.at[y], qa.at[y], q2_s.at[n], q2_r.at[n], plane(d, 0)))
        q2.append(send(qb.at[x], qb.at[x], q2_s.at[n + 3], q2_r.at[n + 3], plane(0, d)))

    for cp in pi:
        cp.wait_recv()
    dall[k, 1 - b] = (drecv[0].astype(F32) + drecv[1].astype(F32)).astype(BF16)
    sw = send(dall.at[k, 1 - b], dall.at[k, 1 - b], sw_s, sw_r, near_far)
    qd = [send(dall.at[k, 1 - b], dall.at[k, 1 - b], qd_s.at[n], qd_r.at[n], quad(n + 1)) for n in range(3)]
    sw.wait_recv()
    qd += [send(dall.at[k, b], dall.at[k, b], qd_s.at[n + 3], qd_r.at[n + 3], quad(n + 1)) for n in range(3)]
    for cp in qd:
        cp.wait_recv()

    wide = [dall[g % 4, g // 4].astype(F32) for g in range(8)]
    docs = jnp.concatenate([w[:8] for w in wide] + [w[8:] for w in wide], axis=0).astype(BF16)
    for cp in q2:
        cp.wait_recv()
    nt = (((1,), (1,)), ((), ()))
    sc_a[...] = lax.dot_general(qa[...].reshape(1024, 1024), docs[:, :1024], nt, preferred_element_type=F32).reshape(4, 4, 64, 128)
    sc_b[...] = lax.dot_general(qb[...].reshape(1024, 1024), docs[:, 1024:], nt, preferred_element_type=F32).reshape(4, 4, 64, 128)

    for gy in range(4):
        for gx in range(4):
            s = sc_a[gy, gx] + sc_b[gx, gy]
            top, bottom = s[:32], s[32:]
            pk[0, gy, gx] = jnp.where(low, top, pltpu.roll(bottom, 64, 1))
            pk[1, gy, gx] = jnp.where(low, pltpu.roll(top, 64, 1), bottom)
    s2 = send(pk.at[1 - c], pk_recv, s2_s, s2_r, sibling)
    s2.wait_recv()
    fin[...] = pk[c] + pk_recv[...]
    os = []
    for n, (dy, dx) in enumerate(offsets):
        os.append(send(
            fin.at[lax.rem(y + dy, 4), lax.rem(x + dx, 4)], fin_recv.at[y, x], o_s.at[n], o_r.at[n], plane(dy, dx)
        ))
    fin_recv[y, x] = fin[y, x]
    for cp in os:
        cp.wait_recv()
    for n in range(8):
        first, second = fin_recv[n // 2, 2 * (n % 2)], fin_recv[n // 2, 2 * (n % 2) + 1]
        out_ref[:32, n * 128:(n + 1) * 128] = jnp.where(low, first, pltpu.roll(second, 64, 1))
        out_ref[32:, n * 128:(n + 1) * 128] = jnp.where(low, pltpu.roll(first, 64, 1), second)

    for cp in [sib, *pi, *q2, sw, *qd, s2, *os]:
        cp.wait_send()


def body(proj_rows, query_features, doc_lengths, owner_map):
    vmem = pl.BlockSpec(memory_space=pltpu.VMEM)
    dma = pltpu.SemaphoreType.DMA
    return pl.pallas_call(
        kernel,
        name="scores",
        out_shape=jax.ShapeDtypeStruct((64, 1024), F32),
        in_specs=[vmem, vmem, vmem, pl.BlockSpec(memory_space=pl.ANY)],
        out_specs=vmem,
        scratch_shapes=[
            pltpu.VMEM((2048, 128), BF16),
            pltpu.VMEM((64, 2048), F32),
            pltpu.VMEM((32, 2048), F32),
            pltpu.VMEM((2, 32, 2048), F32),
            pltpu.VMEM((32, 2048), F32),
            pltpu.VMEM((2, 16, 2048), BF16),
            pltpu.VMEM((2, 16, 2048), BF16),
            pltpu.VMEM((4, 2, 16, 2048), BF16),
            pltpu.VMEM((4, 4, 64, 1024), BF16),
            pltpu.VMEM((4, 4, 64, 1024), BF16),
            pltpu.VMEM((4, 4, 64, 128), F32),
            pltpu.VMEM((4, 4, 64, 128), F32),
            pltpu.VMEM((2, 4, 4, 32, 128), F32),
            pltpu.VMEM((4, 4, 32, 128), F32),
            pltpu.VMEM((4, 4, 32, 128), F32),
            pltpu.VMEM((4, 4, 32, 128), F32),
            dma, dma, dma((6,)), dma((6,)), dma((6,)), dma((6,)), dma((2,)),
            dma((2,)), dma((2,)), dma, dma, dma((6,)), dma((6,)), dma, dma, dma((15,)), dma((15,)),
        ],
        compiler_params=pltpu.CompilerParams(
            collective_id=0, has_side_effects=True, vmem_limit_bytes=48 << 20
        ),
    )(proj_rows, doc_lengths, owner_map, query_features)


def solution(mesh):
    placed = (P(("ex", "tok"), None), P("ex", None), P("ex", None), P("ex", None))
    return jax.shard_map(
        body, mesh=mesh, in_specs=placed, out_specs=P("ex", "tok"), check_vma=False
    )
```

time: 1090 us -> 61.1 us (0.06)
  the two profiles are of different devices: /device:TPU:0 before, /device:TPU:1 now
where the time goes in v1:
time: 61.1 us; the launch traced here: 60.9 us
  Pallas kernels  56.8 us (93%)
  local copies, waits for them, and re-layouts  4.1 us (7%)
    pallas_call x1, Pallas kernels, body(): pl.pallas_call(kernel, name='scores', out_shape=jax.ShapeDtypeStruct((64,...  56.8 us
    unnamed x9, local copies, waits for them, and re-layouts  4.1 us

profile of v1, /device:TPU:1, one launch (start us, length us, event | category | flops | bytes accessed | tf_op | source)
XLA Modules:
  0.0 60.9 jit_solution(4519888772690085886)
XLA Ops:
  0.0 0.0 copy-start
  0.0 1.0 %copy-done = bf16[2048,128]{1,0:T(8,128)(2,1)S(1)} copy-done((bf16[2048,128]{1,0:T(8,128)(2,1)S(1)}, bf16[2048,128]{1,0:T(8,128)(2,1)}, u32[]{:S(2)}) %copy-start) | copy-done | bytes 524312
  1.0 0.0 copy-start.1
  1.0 1.0 %copy-done.1 = bf16[64,4096]{1,0:T(8,128)(2,1)S(1)} copy-done((bf16[64,4096]{1,0:T(8,128)(2,1)S(1)}, bf16[64,4096]{1,0:T(8,128)(2,1)}, u32[]{:S(2)}) %copy-start.1) | copy-done | bytes 524312
  2.1 0.0 copy-start.2
  2.1 0.7 %copy-done.2 = s32[1,32]{1,0:T(1,128)S(1)} copy-done((s32[1,32]{1,0:T(1,128)S(1)}, s32[1,32]{1,0:T(1,128)}, u32[]{:S(2)}) %copy-start.2) | copy-done | bytes 152
  2.7 0.0 copy-start.3
  2.7 0.7 %copy-done.3 = s32[1,32]{1,0:T(1,128)S(1)} copy-done((s32[1,32]{1,0:T(1,128)S(1)}, s32[1,32]{1,0:T(1,128)}, u32[]{:S(2)}) %copy-start.3) | copy-done | bytes 152
  3.4 56.8 %scores.1 = f32[64,1024]{1,0:T(8,128)S(1)} custom-call(bf16[2048,128]{1,0:T(8,128)(2,1)S(1)} %copy-done, s32[1,32]{1,0:T(1,128)S(1)} %copy-done.2, s32[1,32]{1,0:T(1,128)S(1)} %copy-done.3, bf16[64,4096]{1,0:T(8,128)(2,1)S(1)} %copy-done.1), custom_call_target="tpu_custom_call" | custom-call | tf_op jit(solution)/shard_map/scores/pallas_call | solution.py:175
  60.2 0.7 %copy.6 = f32[64,1024]{1,0:T(8,128)} copy(f32[64,1024]{1,0:T(8,128)S(1)} %scores.1) | data formatting | bytes 524288
Async XLA Ops:
  0.0 1.0 %copy-start = (bf16[2048,128]{1,0:T(8,128)(2,1)S(1)}, bf16[2048,128]{1,0:T(8,128)(2,1)}, u32[]{:S(2)}) copy-start(bf16[2048,128]{1,0:T(8,128)(2,1)} %rows_ref.1) | copy-start | bytes 1572868
  1.0 1.0 %copy-start.1 = (bf16[64,4096]{1,0:T(8,128)(2,1)S(1)}, bf16[64,4096]{1,0:T(8,128)(2,1)}, u32[]{:S(2)}) copy-start(bf16[64,4096]{1,0:T(8,128)(2,1)} %q_hbm.1) | copy-start | bytes 1572868
  2.1 0.7 %copy-start.2 = (s32[1,32]{1,0:T(1,128)S(1)}, s32[1,32]{1,0:T(1,128)}, u32[]{:S(2)}) copy-start(s32[1,32]{1,0:T(1,128)} %lens_ref.1) | copy-start | bytes 388
  2.7 0.7 %copy-start.3 = (s32[1,32]{1,0:T(1,128)S(1)}, s32[1,32]{1,0:T(1,128)}, u32[]{:S(2)}) copy-start(s32[1,32]{1,0:T(1,128)} %owner_ref.1) | copy-start | bytes 388

commit v2 on v1

--- a/solution.py
+++ b/solution.py
@@ -11,9 +11,10 @@
 
 
 def kernel(
-    rows_ref, lens_ref, owner_ref, q_hbm, out_ref,
+    rows_hbm, lens_hbm, owner_hbm, q_hbm, out_ref,
+    rows_ref, lens_ref, owner_ref,
     xx, gt, mask, part, sib_recv, dsend, drecv, dall, qa, qb, sc_a, sc_b, pk, pk_recv, fin, fin_recv,
-    sib_s, sib_r, q1_s, q1_r, q2_s, q2_r, ql, pi_s, pi_r, sw_s, sw_r, qd_s, qd_r, s2_s, s2_r, o_s, o_r,
+    in_l, ql, sib_s, sib_r, qs, qr, pi_s, pi_r, sw_s, sw_r, f_s, f_r, g_s, g_r, s2_s, s2_r, o_s, o_r,
 ):
     ex, tok = lax.axis_index("ex"), lax.axis_index("tok")
     y, x, p = ex // 32, lax.rem(ex // 8, 4), lax.rem(ex, 8)
@@ -26,21 +27,30 @@
     def plane(dy, dx):
         return at(lax.rem(y + dy, 4), lax.rem(x + dx, 4), p, h, c)
 
+    loads = [
+        pltpu.make_async_copy(src, dst, in_l.at[n])
+        for n, (src, dst) in enumerate(((lens_hbm, lens_ref), (owner_hbm, owner_ref), (rows_hbm, rows_ref)))
+    ]
+    for cp in loads:
+        cp.start()
+
     far = lax.rem(p + 4, 8)
     sibling = at(y, x, p, h, 1 - c)
     near_far = at(y, x, far, h, c)
     other_far = at(y, x, far, 1 - h, c)
 
-    def quad(d):
-        return at(y, x, b * 4 + lax.rem(k + d, 4), h, c)
+    flip3 = at(y, x, b * 4 + 3 - k, h, c)
+    flip1 = at(y, x, p + 1 - 2 * lax.rem(p, 2), h, c)
 
     offsets = [(dy, dx) for dy in range(4) for dx in range(4) if dy or dx]
-    partners = [plane(*o) for o in offsets] + [quad(d) for d in (1, 2, 3)] + [sibling, near_far, other_far]
+    partners = [plane(*o) for o in offsets] + [flip3, flip1, sibling, near_far, other_far]
 
     barrier = pltpu.get_barrier_semaphore()
     for partner in partners:
         pl.semaphore_signal(barrier, inc=1, device_id=partner, device_id_type=MESH)
 
+    loads[0].wait()
+    loads[1].wait()
     lens = lens_ref[...].astype(F32)
     owner = owner_ref[...]
     lane = lax.broadcasted_iota(jnp.int32, (32, 32), 1)
@@ -55,6 +65,7 @@
     pos = (lax.broadcasted_iota(jnp.int32, (32, 2048), 1) + tok * 2048).astype(F32)
     mask[...] = jnp.where((pos >= begin) & (pos < end), 1.0, 0.0)
 
+    loads[2].wait()
     pick_r = lax.broadcasted_iota(jnp.int32, (64, 128), 0)
     pick_c = lax.broadcasted_iota(jnp.int32, (64, 128), 1)
     pick_g = (pick_c == pick_r + 64).astype(BF16)
@@ -95,16 +106,54 @@
 
     sib = send(part.at[0], sib_recv, sib_s, sib_r, sibling)
 
-    cols_a = pl.ds(pl.multiple_of(c * 2048, 1024), 1024)
-    cols_b = pl.ds(pl.multiple_of(c * 2048 + 1024, 1024), 1024)
-    q1 = []
-    for n, d in enumerate((1, 2, 3)):
-        q1.append(send(q_hbm.at[:, cols_a], qa.at[y, x], q1_s.at[n], q1_r.at[n], plane(0, d)))
-        q1.append(send(q_hbm.at[:, cols_b], qb.at[x, y], q1_s.at[n + 3], q1_r.at[n + 3], plane(d, 0)))
-    own_a = pltpu.make_async_copy(q_hbm.at[:, cols_a], qa.at[y, x], ql.at[0])
-    own_b = pltpu.make_async_copy(q_hbm.at[:, cols_b], qb.at[x, y], ql.at[1])
-    own_a.start()
-    own_b.start()
+    halves = ((qa, y, x, lambda d: plane(0, d), lambda d: plane(d, 0)), (qb, x, y, lambda d: plane(d, 0), lambda d: plane(0, d)))
+    steps = (1, 3)
+
+    started = []
+
+    def q_send(n, src, dst, sem, to):
+        cp = send(src, dst, qs.at[n, sem], qr.at[n, sem], to)
+        started.append(cp)
+        return cp
+
+    parts = (pl.ds(0, 32), pl.ds(32, 32))
+    first, rest = [], []
+    for n, (buf, r, s, ring, cross) in enumerate(halves):
+        cols = pl.ds(pl.multiple_of(c * 2048 + n * 1024, 1024), 1024)
+        own = pltpu.make_async_copy(q_hbm.at[:, cols], buf.at[r, s], ql.at[n])
+        own.start()
+        rest.append(own)
+        for i, d in enumerate(steps):
+            first.append(q_send(n, q_hbm.at[:, cols], buf.at[r, s], i, ring(d)))
+    cross_own = []
+    for n, (buf, r, s, ring, cross) in enumerate(halves):
+        cols = pl.ds(pl.multiple_of(c * 2048 + n * 1024, 1024), 1024)
+        for i, d in enumerate(steps):
+            cross_own.append(q_send(n, q_hbm.at[:, cols], buf.at[r, s], 2 + i, cross(d)))
+
+    def hop_ring():
+        out = []
+        for n, (buf, r, s, ring, cross) in enumerate(halves):
+            for i, d in enumerate(steps):
+                blk = buf.at[r, lax.rem(s + 4 - d, 4), parts[i]]
+                out.append(q_send(n, blk, blk, 4 + i, ring(d)))
+        return out
+
+    def hop_cross(e, base):
+        out = []
+        for n, (buf, r, s, ring, cross) in enumerate(halves):
+            blk = buf.at[r, lax.rem(s + e, 4)]
+            for i, d in enumerate(steps):
+                out.append(q_send(n, blk, blk, base + i, cross(d)))
+        return out
+
+    def hop_cross_on(e, base):
+        out = []
+        for n, (buf, r, s, ring, cross) in enumerate(halves):
+            for i, d in enumerate(steps):
+                blk = buf.at[lax.rem(r + 4 - d, 4), lax.rem(s + e, 4), parts[i]]
+                out.append(q_send(n, blk, blk, base + i, cross(d)))
+        return out
 
     kron_half(c, part.at[1])
     sib.wait_recv()
@@ -116,47 +165,71 @@
         send(dsend.at[1 - h], drecv.at[1], pi_s.at[1], pi_r.at[1], other_far),
     ]
 
-    own_a.wait()
-    own_b.wait()
-    for cp in q1:
+    for cp in first:
+        cp.wait_recv()
+    ring_on = hop_ring()
+    cross_1 = hop_cross(1, 6) + hop_cross(3, 8)
+    for cp in cross_own:
+        cp.wait_recv()
+    on_own = hop_cross_on(0, 10)
+
+    for cp in pi:
+        cp.wait_recv()
+    dall[1 - b, k] = (drecv[0].astype(F32) + drecv[1].astype(F32)).astype(BF16)
+    mine, swapped = dall.at[1 - b, k], dall.at[b, k]
+    sw = send(mine, mine, sw_s, sw_r, near_far)
+    f1 = send(mine, mine, f_s.at[0], f_r.at[0], flip3)
+
+    for cp in ring_on:
+        cp.wait_recv()
+    cross_2 = hop_cross(2, 12)
+    for cp in cross_1:
+        cp.wait_recv()
+    on_1 = hop_cross_on(1, 14) + hop_cross_on(3, 16)
+
+    f1.wait_recv()
+    other = dall.at[1 - b, 3 - k]
+    ones = [send(mine, mine, g_s.at[0], g_r.at[0], flip1), send(other, other, g_s.at[1], g_r.at[1], flip1)]
+    sw.wait_recv()
+    f2 = send(swapped, swapped, f_s.at[1], f_r.at[1], flip3)
+    ones.append(send(swapped, swapped, g_s.at[2], g_r.at[2], flip1))
+    for cp in cross_2:
+        cp.wait_recv()
+    on_2 = hop_cross_on(2, 18)
+    f2.wait_recv()
+    other = dall.at[b, 3 - k]
+    ones.append(send(other, other, g_s.at[3], g_r.at[3], flip1))
+    for cp in rest:
         cp.wait()
-    q2 = []
-    for n, d in enumerate((1, 2, 3)):
-        q2.append(send(qa.at[y], qa.at[y], q2_s.at[n], q2_r.at[n], plane(d, 0)))
-        q2.append(send(qb.at[x], qb.at[x], q2_s.at[n + 3], q2_r.at[n + 3], plane(0, d)))
-
-    for cp in pi:
-        cp.wait_recv()
-    dall[k, 1 - b] = (drecv[0].astype(F32) + drecv[1].astype(F32)).astype(BF16)
-    sw = send(dall.at[k, 1 - b], dall.at[k, 1 - b], sw_s, sw_r, near_far)
-    qd = [send(dall.at[k, 1 - b], dall.at[k, 1 - b], qd_s.at[n], qd_r.at[n], quad(n + 1)) for n in range(3)]
-    sw.wait_recv()
-    qd += [send(dall.at[k, b], dall.at[k, b], qd_s.at[n + 3], qd_r.at[n + 3], quad(n + 1)) for n in range(3)]
-    for cp in qd:
-        cp.wait_recv()
-
-    wide = [dall[g % 4, g // 4].astype(F32) for g in range(8)]
+    for cp in ones:
+        cp.wait_recv()
+
+    wide = [dall[g // 4, g % 4].astype(F32) for g in range(8)]
     docs = jnp.concatenate([w[:8] for w in wide] + [w[8:] for w in wide], axis=0).astype(BF16)
-    for cp in q2:
+    for cp in on_own + on_1 + on_2:
         cp.wait_recv()
     nt = (((1,), (1,)), ((), ()))
+    sc_b[...] = lax.dot_general(qb[...].reshape(1024, 1024), docs[:, 1024:], nt, preferred_element_type=F32).reshape(4, 4, 64, 128)
     sc_a[...] = lax.dot_general(qa[...].reshape(1024, 1024), docs[:, :1024], nt, preferred_element_type=F32).reshape(4, 4, 64, 128)
-    sc_b[...] = lax.dot_general(qb[...].reshape(1024, 1024), docs[:, 1024:], nt, preferred_element_type=F32).reshape(4, 4, 64, 128)
-
-    for gy in range(4):
+
+    s2 = []
+    for n in range(4):
+        gy = lax.rem(y + n + 1, 4)
         for gx in range(4):
-            s = sc_a[gy, gx] + sc_b[gx, gy]
-            top, bottom = s[:32], s[32:]
+            sc = sc_a[gy, gx] + sc_b[gx, gy]
+            top, bottom = sc[:32], sc[32:]
             pk[0, gy, gx] = jnp.where(low, top, pltpu.roll(bottom, 64, 1))
             pk[1, gy, gx] = jnp.where(low, pltpu.roll(top, 64, 1), bottom)
-    s2 = send(pk.at[1 - c], pk_recv, s2_s, s2_r, sibling)
-    s2.wait_recv()
-    fin[...] = pk[c] + pk_recv[...]
+        s2.append(send(pk.at[1 - c, gy], pk_recv.at[gy], s2_s.at[n], s2_r.at[n], sibling))
     os = []
-    for n, (dy, dx) in enumerate(offsets):
-        os.append(send(
-            fin.at[lax.rem(y + dy, 4), lax.rem(x + dx, 4)], fin_recv.at[y, x], o_s.at[n], o_r.at[n], plane(dy, dx)
-        ))
+    for n in range(4):
+        s2[n].wait_recv()
+        gy = lax.rem(y + n + 1, 4)
+        fin[gy] = pk[c, gy] + pk_recv[gy]
+        for dx in range(4):
+            if n < 3 or dx:
+                gx = lax.rem(x + dx, 4)
+                os.append(send(fin.at[gy, gx], fin_recv.at[y, x], o_s.at[n * 4 + dx], o_r.at[n * 4 + dx], plane(n + 1, dx)))
     fin_recv[y, x] = fin[y, x]
     for cp in os:
         cp.wait_recv()
@@ -165,7 +238,7 @@
         out_ref[:32, n * 128:(n + 1) * 128] = jnp.where(low, first, pltpu.roll(second, 64, 1))
         out_ref[32:, n * 128:(n + 1) * 128] = jnp.where(low, pltpu.roll(first, 64, 1), second)
 
-    for cp in [sib, *pi, *q2, sw, *qd, s2, *os]:
+    for cp in [sib, *pi, *started, sw, f1, f2, *ones, *s2, *os]:
         cp.wait_send()
 
 
@@ -176,9 +249,12 @@
         kernel,
         name="scores",
         out_shape=jax.ShapeDtypeStruct((64, 1024), F32),
-        in_specs=[vmem, vmem, vmem, pl.BlockSpec(memory_space=pl.ANY)],
+        in_specs=[pl.BlockSpec(memory_space=pl.ANY)] * 4,
         out_specs=vmem,
         scratch_shapes=[
+            pltpu.VMEM((2048, 128), BF16),
+            pltpu.VMEM((1, 32), jnp.int32),
+            pltpu.VMEM((1, 32), jnp.int32),
             pltpu.VMEM((2048, 128), BF16),
             pltpu.VMEM((64, 2048), F32),
             pltpu.VMEM((32, 2048), F32),
@@ -186,7 +262,7 @@
             pltpu.VMEM((32, 2048), F32),
             pltpu.VMEM((2, 16, 2048), BF16),
             pltpu.VMEM((2, 16, 2048), BF16),
-            pltpu.VMEM((4, 2, 16, 2048), BF16),
+            pltpu.VMEM((2, 4, 16, 2048), BF16),
             pltpu.VMEM((4, 4, 64, 1024), BF16),
             pltpu.VMEM((4, 4, 64, 1024), BF16),
             pltpu.VMEM((4, 4, 64, 128), F32),
@@ -195,8 +271,9 @@
             pltpu.VMEM((4, 4, 32, 128), F32),
             pltpu.VMEM((4, 4, 32, 128), F32),
             pltpu.VMEM((4, 4, 32, 128), F32),
-            dma, dma, dma((6,)), dma((6,)), dma((6,)), dma((6,)), dma((2,)),
-            dma((2,)), dma((2,)), dma, dma, dma((6,)), dma((6,)), dma, dma, dma((15,)), dma((15,)),
+            dma((3,)), dma((2,)), dma, dma, dma((2, 20)), dma((2, 20)),
+            dma((2,)), dma((2,)), dma, dma, dma((2,)), dma((2,)), dma((4,)), dma((4,)),
+            dma((4,)), dma((4,)), dma((16,)), dma((16,)),
         ],
         compiler_params=pltpu.CompilerParams(
             collective_id=0, has_side_effects=True, vmem_limit_bytes=48 << 20

time: 61.1 us -> 54.6 us (0.89)
  the two profiles are of different devices: /device:TPU:1 before, /device:TPU:33 now
where the time goes in v2:
time: 54.6 us; the launch traced here: 54.4 us
  Pallas kernels  50.3 us (92%)
  local copies, waits for them, and re-layouts  4.1 us (8%)
    pallas_call x1, Pallas kernels, body(): pl.pallas_call(kernel, name='scores', out_shape=jax.ShapeDtypeStruct((64,...  50.3 us
    unnamed x9, local copies, waits for them, and re-layouts  4.1 us

profile of v2, /device:TPU:33, one launch (start us, length us, event | category | flops | bytes accessed | tf_op | source)
XLA Modules:
  0.0 54.4 jit_solution(11094723937487619017)
XLA Ops:
  0.0 0.0 copy-start
  0.0 1.0 %copy-done = bf16[2048,128]{1,0:T(8,128)(2,1)S(1)} copy-done((bf16[2048,128]{1,0:T(8,128)(2,1)S(1)}, bf16[2048,128]{1,0:T(8,128)(2,1)}, u32[]{:S(2)}) %copy-start) | copy-done | bytes 524312
  1.0 0.0 copy-start.1
  1.0 1.0 %copy-done.1 = bf16[64,4096]{1,0:T(8,128)(2,1)S(1)} copy-done((bf16[64,4096]{1,0:T(8,128)(2,1)S(1)}, bf16[64,4096]{1,0:T(8,128)(2,1)}, u32[]{:S(2)}) %copy-start.1) | copy-done | bytes 524312
  2.1 0.0 copy-start.2
  2.1 0.7 %copy-done.2 = s32[1,32]{1,0:T(1,128)S(1)} copy-done((s32[1,32]{1,0:T(1,128)S(1)}, s32[1,32]{1,0:T(1,128)}, u32[]{:S(2)}) %copy-start.2) | copy-done | bytes 152
  2.7 0.0 copy-start.3
  2.7 0.7 %copy-done.3 = s32[1,32]{1,0:T(1,128)S(1)} copy-done((s32[1,32]{1,0:T(1,128)S(1)}, s32[1,32]{1,0:T(1,128)}, u32[]{:S(2)}) %copy-start.3) | copy-done | bytes 152
  3.4 50.3 %scores.1 = f32[64,1024]{1,0:T(8,128)S(1)} custom-call(bf16[2048,128]{1,0:T(8,128)(2,1)S(1)} %copy-done, s32[1,32]{1,0:T(1,128)S(1)} %copy-done.2, s32[1,32]{1,0:T(1,128)S(1)} %copy-done.3, bf16[64,4096]{1,0:T(8,128)(2,1)S(1)} %copy-done.1), custom_call_target="tpu_custom_call" | custom-call | tf_op jit(solution)/shard_map/scores/pallas_call | solution.py:248
  53.7 0.7 %copy.6 = f32[64,1024]{1,0:T(8,128)} copy(f32[64,1024]{1,0:T(8,128)S(1)} %scores.1) | data formatting | bytes 524288
Async XLA Ops:
  0.0 1.0 %copy-start = (bf16[2048,128]{1,0:T(8,128)(2,1)S(1)}, bf16[2048,128]{1,0:T(8,128)(2,1)}, u32[]{:S(2)}) copy-start(bf16[2048,128]{1,0:T(8,128)(2,1)} %rows_hbm.1) | copy-start | bytes 1572868
  1.0 1.0 %copy-start.1 = (bf16[64,4096]{1,0:T(8,128)(2,1)S(1)}, bf16[64,4096]{1,0:T(8,128)(2,1)}, u32[]{:S(2)}) copy-start(bf16[64,4096]{1,0:T(8,128)(2,1)} %q_hbm.1) | copy-start | bytes 1572868
  2.1 0.7 %copy-start.2 = (s32[1,32]{1,0:T(1,128)S(1)}, s32[1,32]{1,0:T(1,128)}, u32[]{:S(2)}) copy-start(s32[1,32]{1,0:T(1,128)} %lens_hbm.1) | copy-start | bytes 388
  2.7 0.7 %copy-start.3 = (s32[1,32]{1,0:T(1,128)S(1)}, s32[1,32]{1,0:T(1,128)}, u32[]{:S(2)}) copy-start(s32[1,32]{1,0:T(1,128)} %owner_hbm.1) | copy-start | bytes 388

commit v3 on v2

--- a/solution.py
+++ b/solution.py
@@ -13,7 +13,7 @@
 def kernel(
     rows_hbm, lens_hbm, owner_hbm, q_hbm, out_ref,
     rows_ref, lens_ref, owner_ref,
-    xx, gt, mask, part, sib_recv, dsend, drecv, dall, qa, qb, sc_a, sc_b, pk, pk_recv, fin, fin_recv,
+    gt, mask, part, sib_recv, dsend, drecv, dall, qa, qb, sc_a, sc_b, pk, pk_recv, fin, fin_recv,
     in_l, ql, sib_s, sib_r, qs, qr, pi_s, pi_r, sw_s, sw_r, f_s, f_r, g_s, g_r, s2_s, s2_r, o_s, o_r,
 ):
     ex, tok = lax.axis_index("ex"), lax.axis_index("tok")
@@ -43,7 +43,7 @@
     flip1 = at(y, x, p + 1 - 2 * lax.rem(p, 2), h, c)
 
     offsets = [(dy, dx) for dy in range(4) for dx in range(4) if dy or dx]
-    partners = [plane(*o) for o in offsets] + [flip3, flip1, sibling, near_far, other_far]
+    partners = [plane(0, 1), plane(0, 3), plane(1, 0), plane(3, 0)] + [flip3, flip1, sibling, near_far, other_far]
 
     barrier = pltpu.get_barrier_semaphore()
     for partner in partners:
@@ -63,38 +63,31 @@
     end = begin + size
     scale = 1.0 / jnp.sqrt(size)
     pos = (lax.broadcasted_iota(jnp.int32, (32, 2048), 1) + tok * 2048).astype(F32)
-    mask[...] = jnp.where((pos >= begin) & (pos < end), 1.0, 0.0)
+    mask[...] = jnp.where((pos >= begin) & (pos < end), 1.0, 0.0).astype(BF16)
 
     loads[2].wait()
     pick_r = lax.broadcasted_iota(jnp.int32, (64, 128), 0)
     pick_c = lax.broadcasted_iota(jnp.int32, (64, 128), 1)
     pick_g = (pick_c == pick_r + 64).astype(BF16)
     gt[...] = lax.dot_general(pick_g, rows_ref[...], (((1,), (1,)), ((), ())), preferred_element_type=F32)
-    twice_r = lax.broadcasted_iota(jnp.int32, (128, 128), 0)
-    twice_c = lax.broadcasted_iota(jnp.int32, (128, 128), 1)
-    twice = ((twice_r == twice_c) | (twice_r + 64 == twice_c)).astype(F32)
-    twice = jnp.where(twice_r < 64, twice, 0.0).astype(BF16)
-    xx[...] = jnp.dot(rows_ref[...], twice, preferred_element_type=F32).astype(BF16)
 
     low = lax.broadcasted_iota(jnp.int32, (32, 128), 1) < 64
 
     def kron_half(half, dest):
-        def step(n, carry):
+        for n in range(2):
             blocks = []
             for i in range(16):
-                g_row = gt[pl.ds(half * 32 + n * 16 + i, 1), :]
-                blocks.append((mask[...] * g_row).astype(BF16))
+                g_row = jnp.broadcast_to(gt[pl.ds(half * 32 + n * 16 + i, 1), :], (16, 2048)).astype(BF16)
+                blocks += [mask[:16] * g_row, mask[16:] * g_row]
             spread = jnp.concatenate(blocks, axis=0)
-            res = jnp.dot(spread, xx[...], preferred_element_type=F32)
+            res = jnp.dot(spread, rows_ref[...], preferred_element_type=F32)
             for i in range(8):
                 even = res[64 * i:64 * i + 32]
-                odd = res[64 * i + 32:64 * i + 64]
-                dest[:, pl.ds(pl.multiple_of((n * 8 + i) * 128, 128), 128)] = jnp.where(low, even, odd)
-            return carry
-
-        lax.fori_loop(0, 2, step, 0)
+                odd = pltpu.roll(res[64 * i + 32:64 * i + 64], 64, 1)
+                dest[n, :, i * 128:(i + 1) * 128] = jnp.where(low, even, odd)
 
     kron_half(1 - c, part.at[0])
+    kron_half(c, part.at[1])
     pl.semaphore_wait(barrier, len(partners))
 
     def send(src, dst, ss, rs, to):
@@ -104,7 +97,7 @@
         cp.start()
         return cp
 
-    sib = send(part.at[0], sib_recv, sib_s, sib_r, sibling)
+    sib = [send(part.at[0, n], sib_recv.at[n], sib_s.at[n], sib_r.at[n], sibling) for n in range(2)]
 
     halves = ((qa, y, x, lambda d: plane(0, d), lambda d: plane(d, 0)), (qb, x, y, lambda d: plane(d, 0), lambda d: plane(0, d)))
     steps = (1, 3)
@@ -155,15 +148,43 @@
                 out.append(q_send(n, blk, blk, base + i, cross(d)))
         return out
 
-    kron_half(c, part.at[1])
-    sib.wait_recv()
-    feats = ((part[1] + sib_recv[...]) * scale).astype(BF16)
-    dsend[0] = feats[:16]
-    dsend[1] = feats[16:]
-    pi = [
-        send(dsend.at[h], drecv.at[0], pi_s.at[0], pi_r.at[0], near_far),
-        send(dsend.at[1 - h], drecv.at[1], pi_s.at[1], pi_r.at[1], other_far),
-    ]
+    pi = []
+    for n in range(2):
+        sib[n].wait_recv()
+        feats = ((part[1, n] + sib_recv[n]) * scale).astype(BF16)
+        dsend[n, 0] = feats[:16]
+        dsend[n, 1] = feats[16:]
+        pi.append([
+            send(dsend.at[n, h], drecv.at[n, 0], pi_s.at[n, 0], pi_r.at[n, 0], near_far),
+            send(dsend.at[n, 1 - h], drecv.at[n, 1], pi_s.at[n, 1], pi_r.at[n, 1], other_far),
+        ])
+
+    swaps, threes, ones = [], [], []
+
+    def meet(n):
+        for cp in pi[n]:
+            cp.wait_recv()
+        dall[n, 1 - b, k] = (drecv[n, 0].astype(F32) + drecv[n, 1].astype(F32)).astype(BF16)
+        mine = dall.at[n, 1 - b, k]
+        swaps.append(send(mine, mine, sw_s.at[n], sw_r.at[n], near_far))
+        threes.append(send(mine, mine, f_s.at[n, 0], f_r.at[n, 0], flip3))
+        ones.append(send(mine, mine, g_s.at[n, 0], g_r.at[n, 0], flip1))
+
+    def far_one(n):
+        threes[n].wait_recv()
+        blk = dall.at[n, 1 - b, 3 - k]
+        ones.append(send(blk, blk, g_s.at[n, 1], g_r.at[n, 1], flip1))
+
+    def swapped(n):
+        swaps[n].wait_recv()
+        blk = dall.at[n, b, k]
+        threes.append(send(blk, blk, f_s.at[n, 1], f_r.at[n, 1], flip3))
+        ones.append(send(blk, blk, g_s.at[n, 2], g_r.at[n, 2], flip1))
+
+    def far_two(n):
+        threes[2 + n].wait_recv()
+        blk = dall.at[n, b, 3 - k]
+        ones.append(send(blk, blk, g_s.at[n, 3], g_r.at[n, 3], flip1))
 
     for cp in first:
         cp.wait_recv()
@@ -172,45 +193,37 @@
     for cp in cross_own:
         cp.wait_recv()
     on_own = hop_cross_on(0, 10)
-
-    for cp in pi:
-        cp.wait_recv()
-    dall[1 - b, k] = (drecv[0].astype(F32) + drecv[1].astype(F32)).astype(BF16)
-    mine, swapped = dall.at[1 - b, k], dall.at[b, k]
-    sw = send(mine, mine, sw_s, sw_r, near_far)
-    f1 = send(mine, mine, f_s.at[0], f_r.at[0], flip3)
-
+    meet(0)
     for cp in ring_on:
         cp.wait_recv()
     cross_2 = hop_cross(2, 12)
+    meet(1)
     for cp in cross_1:
         cp.wait_recv()
     on_1 = hop_cross_on(1, 14) + hop_cross_on(3, 16)
-
-    f1.wait_recv()
-    other = dall.at[1 - b, 3 - k]
-    ones = [send(mine, mine, g_s.at[0], g_r.at[0], flip1), send(other, other, g_s.at[1], g_r.at[1], flip1)]
-    sw.wait_recv()
-    f2 = send(swapped, swapped, f_s.at[1], f_r.at[1], flip3)
-    ones.append(send(swapped, swapped, g_s.at[2], g_r.at[2], flip1))
+    far_one(0)
+    swapped(0)
+    far_one(1)
+    swapped(1)
     for cp in cross_2:
         cp.wait_recv()
     on_2 = hop_cross_on(2, 18)
-    f2.wait_recv()
-    other = dall.at[b, 3 - k]
-    ones.append(send(other, other, g_s.at[3], g_r.at[3], flip1))
+    far_two(0)
+    far_two(1)
     for cp in rest:
         cp.wait()
     for cp in ones:
         cp.wait_recv()
 
-    wide = [dall[g // 4, g % 4].astype(F32) for g in range(8)]
-    docs = jnp.concatenate([w[:8] for w in wide] + [w[8:] for w in wide], axis=0).astype(BF16)
+    docs = []
+    for n in range(2):
+        wide = [dall[n, g // 4, g % 4].astype(F32) for g in range(8)]
+        docs.append(jnp.concatenate([w[:8] for w in wide] + [w[8:] for w in wide], axis=0).astype(BF16))
     for cp in on_own + on_1 + on_2:
         cp.wait_recv()
     nt = (((1,), (1,)), ((), ()))
-    sc_b[...] = lax.dot_general(qb[...].reshape(1024, 1024), docs[:, 1024:], nt, preferred_element_type=F32).reshape(4, 4, 64, 128)
-    sc_a[...] = lax.dot_general(qa[...].reshape(1024, 1024), docs[:, :1024], nt, preferred_element_type=F32).reshape(4, 4, 64, 128)
+    sc_b[...] = lax.dot_general(qb[...].reshape(1024, 1024), docs[1], nt, preferred_element_type=F32).reshape(4, 4, 64, 128)
+    sc_a[...] = lax.dot_general(qa[...].reshape(1024, 1024), docs[0], nt, preferred_element_type=F32).reshape(4, 4, 64, 128)
 
     s2 = []
     for n in range(4):
@@ -238,7 +251,7 @@
         out_ref[:32, n * 128:(n + 1) * 128] = jnp.where(low, first, pltpu.roll(second, 64, 1))
         out_ref[32:, n * 128:(n + 1) * 128] = jnp.where(low, pltpu.roll(first, 64, 1), second)
 
-    for cp in [sib, *pi, *started, sw, f1, f2, *ones, *s2, *os]:
+    for cp in [*sib, *pi[0], *pi[1], *started, *swaps, *threes, *ones, *s2, *os]:
         cp.wait_send()
 
 
@@ -255,14 +268,13 @@
             pltpu.VMEM((2048, 128), BF16),
             pltpu.VMEM((1, 32), jnp.int32),
             pltpu.VMEM((1, 32), jnp.int32),
-            pltpu.VMEM((2048, 128), BF16),
             pltpu.VMEM((64, 2048), F32),
-            pltpu.VMEM((32, 2048), F32),
-            pltpu.VMEM((2, 32, 2048), F32),
-            pltpu.VMEM((32, 2048), F32),
-            pltpu.VMEM((2, 16, 2048), BF16),
-            pltpu.VMEM((2, 16, 2048), BF16),
-            pltpu.VMEM((2, 4, 16, 2048), BF16),
+            pltpu.VMEM((32, 2048), BF16),
+            pltpu.VMEM((2, 2, 32, 1024), F32),
+            pltpu.VMEM((2, 32, 1024), F32),
+            pltpu.VMEM((2, 2, 16, 1024), BF16),
+            pltpu.VMEM((2, 2, 16, 1024), BF16),
+            pltpu.VMEM((2, 2, 4, 16, 1024), BF16),
             pltpu.VMEM((4, 4, 64, 1024), BF16),
             pltpu.VMEM((4, 4, 64, 1024), BF16),
             pltpu.VMEM((4, 4, 64, 128), F32),
@@ -271,12 +283,12 @@
             pltpu.VMEM((4, 4, 32, 128), F32),
             pltpu.VMEM((4, 4, 32, 128), F32),
             pltpu.VMEM((4, 4, 32, 128), F32),
-            dma((3,)), dma((2,)), dma, dma, dma((2, 20)), dma((2, 20)),
-            dma((2,)), dma((2,)), dma, dma, dma((2,)), dma((2,)), dma((4,)), dma((4,)),
+            dma((3,)), dma((2,)), dma((2,)), dma((2,)), dma((2, 20)), dma((2, 20)),
+            dma((2, 2)), dma((2, 2)), dma((2,)), dma((2,)), dma((2, 2)), dma((2, 2)), dma((2, 4)), dma((2, 4)),
             dma((4,)), dma((4,)), dma((16,)), dma((16,)),
         ],
         compiler_params=pltpu.CompilerParams(
-            collective_id=0, has_side_effects=True, vmem_limit_bytes=48 << 20
+            collective_id=0, has_side_effects=True, vmem_limit_bytes=64 << 20
         ),
     )(proj_rows, doc_lengths, owner_map, query_features)
 

time: 54.6 us -> 51.4 us (0.941)
  the two profiles are of different devices: /device:TPU:33 before, /device:TPU:1 now
where the time goes in v3:
time: 51.4 us; the launch traced here: 51.1 us
  Pallas kernels  49.4 us (96%)
  local copies, waits for them, and re-layouts  1.67 us (3%)
    pallas_call x1, Pallas kernels, body(): pl.pallas_call(kernel, name='scores', out_shape=jax.ShapeDtypeStruct((64,...  49.4 us
    unnamed x1, local copies, waits for them, and re-layouts  1.67 us

profile of v3, /device:TPU:1, one launch (start us, length us, event | category | flops | bytes accessed | tf_op | source)
XLA Modules:
  0.0 51.1 jit_solution(3674600196947776209)
XLA Ops:
  0.0 49.4 %scores.1 = f32[64,1024]{1,0:T(8,128)} custom-call(bf16[2048,128]{1,0:T(8,128)(2,1)} %rows_hbm.1, s32[1,32]{1,0:T(1,128)} %lens_hbm.1, s32[1,32]{1,0:T(1,128)} %owner_hbm.1, bf16[64,4096]{1,0:T(8,128)(2,1)} %q_hbm.1), custom_call_target="tpu_custom_call" | custom-call | tf_op jit(solution)/shard_map/scores/pallas_call | solution.py:261
  49.5 1.7 %copy.6 = f32[64,1024]{1,0:T(8,128)} copy(f32[64,1024]{1,0:T(8,128)} %scores.1) | data formatting | bytes 524288

commit v4 on v3

--- a/solution.py
+++ b/solution.py
@@ -13,8 +13,8 @@
 def kernel(
     rows_hbm, lens_hbm, owner_hbm, q_hbm, out_ref,
     rows_ref, lens_ref, owner_ref,
-    gt, mask, part, sib_recv, dsend, drecv, dall, qa, qb, sc_a, sc_b, pk, pk_recv, fin, fin_recv,
-    in_l, ql, sib_s, sib_r, qs, qr, pi_s, pi_r, sw_s, sw_r, f_s, f_r, g_s, g_r, s2_s, s2_r, o_s, o_r,
+    gt, mask, part, sib_recv, dsend, drecv, dall, qa, qb, pk, pk_recv, fin, fin_recv,
+    in_l, ql, sib_s, sib_r, qs, qr, pi_s, pi_r, sw_s, sw_r, f_s, f_r, g_s, g_r, s2_s, s2_r, o_s, o_r, ready,
 ):
     ex, tok = lax.axis_index("ex"), lax.axis_index("tok")
     y, x, p = ex // 32, lax.rem(ex // 8, 4), lax.rem(ex, 8)
@@ -42,8 +42,13 @@
     flip3 = at(y, x, b * 4 + 3 - k, h, c)
     flip1 = at(y, x, p + 1 - 2 * lax.rem(p, 2), h, c)
 
-    offsets = [(dy, dx) for dy in range(4) for dx in range(4) if dy or dx]
-    partners = [plane(0, 1), plane(0, 3), plane(1, 0), plane(3, 0)] + [flip3, flip1, sibling, near_far, other_far]
+    z = h * 8 + p
+
+    def along(d):
+        zz = lax.rem(z + 16 + d, 16)
+        return at(y, x, lax.rem(zz, 8), zz // 8, c)
+
+    partners = [plane(0, 1), plane(0, 3), plane(1, 0), plane(3, 0), flip1, sibling, along(2), along(-2)]
 
     barrier = pltpu.get_barrier_semaphore()
     for partner in partners:
@@ -86,9 +91,9 @@
                 odd = pltpu.roll(res[64 * i + 32:64 * i + 64], 64, 1)
                 dest[n, :, i * 128:(i + 1) * 128] = jnp.where(low, even, odd)
 
-    kron_half(1 - c, part.at[0])
-    kron_half(c, part.at[1])
     pl.semaphore_wait(barrier, len(partners))
+    pl.semaphore_signal(ready.at[0], inc=1, device_id=along(2), device_id_type=MESH)
+    pl.semaphore_signal(ready.at[1], inc=1, device_id=along(-2), device_id_type=MESH)
 
     def send(src, dst, ss, rs, to):
         cp = pltpu.make_async_remote_copy(
@@ -96,8 +101,6 @@
         )
         cp.start()
         return cp
-
-    sib = [send(part.at[0, n], sib_recv.at[n], sib_s.at[n], sib_r.at[n], sibling) for n in range(2)]
 
     halves = ((qa, y, x, lambda d: plane(0, d), lambda d: plane(d, 0)), (qb, x, y, lambda d: plane(d, 0), lambda d: plane(0, d)))
     steps = (1, 3)
@@ -148,9 +151,16 @@
                 out.append(q_send(n, blk, blk, base + i, cross(d)))
         return out
 
+    kron_half(1 - c, part.at[0])
+    sib = [send(part.at[0, n], sib_recv.at[n], sib_s.at[n], sib_r.at[n], sibling) for n in range(2)]
+
+    kron_half(c, part.at[1])
     pi = []
     for n in range(2):
         sib[n].wait_recv()
+        if n == 0:
+            pl.semaphore_wait(ready.at[0], 1)
+            pl.semaphore_wait(ready.at[1], 1)
         feats = ((part[1, n] + sib_recv[n]) * scale).astype(BF16)
         dsend[n, 0] = feats[:16]
         dsend[n, 1] = feats[16:]
@@ -222,28 +232,36 @@
     for cp in on_own + on_1 + on_2:
         cp.wait_recv()
     nt = (((1,), (1,)), ((), ()))
-    sc_b[...] = lax.dot_general(qb[...].reshape(1024, 1024), docs[1], nt, preferred_element_type=F32).reshape(4, 4, 64, 128)
-    sc_a[...] = lax.dot_general(qa[...].reshape(1024, 1024), docs[0], nt, preferred_element_type=F32).reshape(4, 4, 64, 128)
-
-    s2 = []
-    for n in range(4):
-        gy = lax.rem(y + n + 1, 4)
+    s2, os = [], []
+    turn = (2, 1, 3, 0)
+
+    def multiply(n):
+        gy = lax.rem(y + turn[n], 4)
+        sc = lax.dot_general(qa[gy].reshape(256, 1024), docs[0], nt, preferred_element_type=F32)
+        sc = sc + lax.dot_general(qb[:, gy].reshape(256, 1024), docs[1], nt, preferred_element_type=F32)
         for gx in range(4):
-            sc = sc_a[gy, gx] + sc_b[gx, gy]
-            top, bottom = sc[:32], sc[32:]
-            pk[0, gy, gx] = jnp.where(low, top, pltpu.roll(bottom, 64, 1))
-            pk[1, gy, gx] = jnp.where(low, pltpu.roll(top, 64, 1), bottom)
-        s2.append(send(pk.at[1 - c, gy], pk_recv.at[gy], s2_s.at[n], s2_r.at[n], sibling))
-    os = []
-    for n in range(4):
+            top, bottom = sc[64 * gx:64 * gx + 32], sc[64 * gx + 32:64 * gx + 64]
+            pk[0, n, gx] = jnp.where(low, top, pltpu.roll(bottom, 64, 1))
+            pk[1, n, gx] = jnp.where(low, pltpu.roll(top, 64, 1), bottom)
+        s2.append(send(pk.at[1 - c, n], pk_recv.at[n], s2_s.at[n], s2_r.at[n], sibling))
+
+    def finish(n):
         s2[n].wait_recv()
-        gy = lax.rem(y + n + 1, 4)
-        fin[gy] = pk[c, gy] + pk_recv[gy]
-        for dx in range(4):
-            if n < 3 or dx:
+        fin[n] = pk[c, n] + pk_recv[n]
+        for dx in turn:
+            if turn[n] or dx:
                 gx = lax.rem(x + dx, 4)
-                os.append(send(fin.at[gy, gx], fin_recv.at[y, x], o_s.at[n * 4 + dx], o_r.at[n * 4 + dx], plane(n + 1, dx)))
-    fin_recv[y, x] = fin[y, x]
+                os.append(send(fin.at[n, gx], fin_recv.at[y, x], o_s.at[n, dx], o_r.at[n, dx], plane(turn[n], dx)))
+
+    multiply(0)
+    multiply(1)
+    finish(0)
+    multiply(2)
+    finish(1)
+    multiply(3)
+    finish(2)
+    finish(3)
+    fin_recv[y, x] = fin[3, x]
     for cp in os:
         cp.wait_recv()
     for n in range(8):
@@ -277,15 +295,13 @@
             pltpu.VMEM((2, 2, 4, 16, 1024), BF16),
             pltpu.VMEM((4, 4, 64, 1024), BF16),
             pltpu.VMEM((4, 4, 64, 1024), BF16),
-            pltpu.VMEM((4, 4, 64, 128), F32),
-            pltpu.VMEM((4, 4, 64, 128), F32),
             pltpu.VMEM((2, 4, 4, 32, 128), F32),
             pltpu.VMEM((4, 4, 32, 128), F32),
             pltpu.VMEM((4, 4, 32, 128), F32),
             pltpu.VMEM((4, 4, 32, 128), F32),
             dma((3,)), dma((2,)), dma((2,)), dma((2,)), dma((2, 20)), dma((2, 20)),
             dma((2, 2)), dma((2, 2)), dma((2,)), dma((2,)), dma((2, 2)), dma((2, 2)), dma((2, 4)), dma((2, 4)),
-            dma((4,)), dma((4,)), dma((16,)), dma((16,)),
+            dma((4,)), dma((4,)), dma((4, 4)), dma((4, 4)), pltpu.SemaphoreType.REGULAR((2,)),
         ],
         compiler_params=pltpu.CompilerParams(
             collective_id=0, has_side_effects=True, vmem_limit_bytes=64 << 20

time: 51.4 us -> 50.6 us (0.984)
  Pallas kernels: 49.4 us -> 48.4 us
    pallas_call x1, Pallas kernels: 49.4 us -> 48.4 us  [body(): pl.pallas_call(kernel, name='scores', out_shape=jax.ShapeDtypeStruct((64,...]
where the time goes in v4:
time: 50.6 us; the launch traced here: 50.1 us
  Pallas kernels  48.4 us (96%)
  local copies, waits for them, and re-layouts  1.67 us (3%)
    pallas_call x1, Pallas kernels, body(): pl.pallas_call(kernel, name='scores', out_shape=jax.ShapeDtypeStruct((64,...  48.4 us
    unnamed x1, local copies, waits for them, and re-layouts  1.67 us

profile of v4, /device:TPU:1, one launch (start us, length us, event | category | flops | bytes accessed | tf_op | source)
XLA Modules:
  0.0 50.1 jit_solution(5693418376278358091)
XLA Ops:
  0.0 48.4 %scores.1 = f32[64,1024]{1,0:T(8,128)} custom-call(bf16[2048,128]{1,0:T(8,128)(2,1)} %rows_hbm.1, s32[1,32]{1,0:T(1,128)} %lens_hbm.1, s32[1,32]{1,0:T(1,128)} %owner_hbm.1, bf16[64,4096]{1,0:T(8,128)(2,1)} %q_hbm.1), custom_call_target="tpu_custom_call" | custom-call | tf_op jit(solution)/shard_map/scores/pallas_call | solution.py:279
  48.4 1.7 %copy.6 = f32[64,1024]{1,0:T(8,128)} copy(f32[64,1024]{1,0:T(8,128)} %scores.1) | data formatting | bytes 524288

commit v5 on v4

--- a/solution.py
+++ b/solution.py
@@ -13,7 +13,7 @@
 def kernel(
     rows_hbm, lens_hbm, owner_hbm, q_hbm, out_ref,
     rows_ref, lens_ref, owner_ref,
-    gt, mask, part, sib_recv, dsend, drecv, dall, qa, qb, pk, pk_recv, fin, fin_recv,
+    gt, mask, part, sib_recv, dsend, drecv, dall, qa, qb, sc_a, pk, pk_recv, fin, fin_recv,
     in_l, ql, sib_s, sib_r, qs, qr, pi_s, pi_r, sw_s, sw_r, f_s, f_r, g_s, g_r, s2_s, s2_r, o_s, o_r, ready,
 ):
     ex, tok = lax.axis_index("ex"), lax.axis_index("tok")
@@ -169,7 +169,7 @@
             send(dsend.at[n, 1 - h], drecv.at[n, 1], pi_s.at[n, 1], pi_r.at[n, 1], other_far),
         ])
 
-    swaps, threes, ones = [], [], []
+    swaps, threes, ones, late = [], [], [], []
 
     def meet(n):
         for cp in pi[n]:
@@ -178,23 +178,23 @@
         mine = dall.at[n, 1 - b, k]
         swaps.append(send(mine, mine, sw_s.at[n], sw_r.at[n], near_far))
         threes.append(send(mine, mine, f_s.at[n, 0], f_r.at[n, 0], flip3))
-        ones.append(send(mine, mine, g_s.at[n, 0], g_r.at[n, 0], flip1))
+        (late if n else ones).append(send(mine, mine, g_s.at[n, 0], g_r.at[n, 0], flip1))
 
     def far_one(n):
         threes[n].wait_recv()
         blk = dall.at[n, 1 - b, 3 - k]
-        ones.append(send(blk, blk, g_s.at[n, 1], g_r.at[n, 1], flip1))
+        (late if n else ones).append(send(blk, blk, g_s.at[n, 1], g_r.at[n, 1], flip1))
 
     def swapped(n):
         swaps[n].wait_recv()
         blk = dall.at[n, b, k]
         threes.append(send(blk, blk, f_s.at[n, 1], f_r.at[n, 1], flip3))
-        ones.append(send(blk, blk, g_s.at[n, 2], g_r.at[n, 2], flip1))
+        (late if n else ones).append(send(blk, blk, g_s.at[n, 2], g_r.at[n, 2], flip1))
 
     def far_two(n):
         threes[2 + n].wait_recv()
         blk = dall.at[n, b, 3 - k]
-        ones.append(send(blk, blk, g_s.at[n, 3], g_r.at[n, 3], flip1))
+        (late if n else ones).append(send(blk, blk, g_s.at[n, 3], g_r.at[n, 3], flip1))
 
     for cp in first:
         cp.wait_recv()
@@ -222,23 +222,35 @@
     far_two(1)
     for cp in rest:
         cp.wait()
+
+    def documents(n):
+        wide = [dall[n, g // 4, g % 4].astype(F32) for g in range(8)]
+        return jnp.concatenate([w[:8] for w in wide] + [w[8:] for w in wide], axis=0).T.astype(BF16)
+
+    turn = (2, 1, 3, 0)
+    nn = (((1,), (0,)), ((), ()))
+
+    def early(n):
+        sc_a[n] = lax.dot_general(qa[lax.rem(y + turn[n], 4)].reshape(256, 1024), docs_a, nn, preferred_element_type=F32)
+
     for cp in ones:
         cp.wait_recv()
-
-    docs = []
-    for n in range(2):
-        wide = [dall[n, g // 4, g % 4].astype(F32) for g in range(8)]
-        docs.append(jnp.concatenate([w[:8] for w in wide] + [w[8:] for w in wide], axis=0).astype(BF16))
-    for cp in on_own + on_1 + on_2:
-        cp.wait_recv()
-    nt = (((1,), (1,)), ((), ()))
+    docs_a = documents(0)
+    for cp in on_own + on_1:
+        cp.wait_recv()
+    early(1)
+    early(2)
+    early(3)
+    for cp in on_2:
+        cp.wait_recv()
+    early(0)
+    for cp in late:
+        cp.wait_recv()
+    docs_b = documents(1)
     s2, os = [], []
-    turn = (2, 1, 3, 0)
-
     def multiply(n):
         gy = lax.rem(y + turn[n], 4)
-        sc = lax.dot_general(qa[gy].reshape(256, 1024), docs[0], nt, preferred_element_type=F32)
-        sc = sc + lax.dot_general(qb[:, gy].reshape(256, 1024), docs[1], nt, preferred_element_type=F32)
+        sc = sc_a[n] + lax.dot_general(qb[:, gy].reshape(256, 1024), docs_b, nn, preferred_element_type=F32)
         for gx in range(4):
             top, bottom = sc[64 * gx:64 * gx + 32], sc[64 * gx + 32:64 * gx + 64]
             pk[0, n, gx] = jnp.where(low, top, pltpu.roll(bottom, 64, 1))
@@ -269,7 +281,7 @@
         out_ref[:32, n * 128:(n + 1) * 128] = jnp.where(low, first, pltpu.roll(second, 64, 1))
         out_ref[32:, n * 128:(n + 1) * 128] = jnp.where(low, pltpu.roll(first, 64, 1), second)
 
-    for cp in [*sib, *pi[0], *pi[1], *started, *swaps, *threes, *ones, *s2, *os]:
+    for cp in [*sib, *pi[0], *pi[1], *started, *swaps, *threes, *ones, *late, *s2, *os]:
         cp.wait_send()
 
 
@@ -295,6 +307,7 @@
             pltpu.VMEM((2, 2, 4, 16, 1024), BF16),
             pltpu.VMEM((4, 4, 64, 1024), BF16),
             pltpu.VMEM((4, 4, 64, 1024), BF16),
+            pltpu.VMEM((4, 256, 128), F32),
             pltpu.VMEM((2, 4, 4, 32, 128), F32),
             pltpu.VMEM((4, 4, 32, 128), F32),
             pltpu.VMEM((4, 4, 32, 128), F32),

time: 50.6 us -> 49.8 us (0.984)
  no operation moved by 1% of the time
where the time goes in v5:
time: 49.8 us; the launch traced here: 49.6 us
  Pallas kernels  47.9 us (96%)
  local copies, waits for them, and re-layouts  1.67 us (3%)
    pallas_call x1, Pallas kernels, body(): pl.pallas_call(kernel, name='scores', out_shape=jax.ShapeDtypeStruct((64,...  47.9 us
    unnamed x1, local copies, waits for them, and re-layouts  1.67 us

profile of v5, /device:TPU:1, one launch (start us, length us, event | category | flops | bytes accessed | tf_op | source)
XLA Modules:
  0.0 49.6 jit_solution(17607178019035671801)
XLA Ops:
  0.0 47.9 %scores.1 = f32[64,1024]{1,0:T(8,128)} custom-call(bf16[2048,128]{1,0:T(8,128)(2,1)} %rows_hbm.1, s32[1,32]{1,0:T(1,128)} %lens_hbm.1, s32[1,32]{1,0:T(1,128)} %owner_hbm.1, bf16[64,4096]{1,0:T(8,128)(2,1)} %q_hbm.1), custom_call_target="tpu_custom_call" | custom-call | tf_op jit(solution)/shard_map/scores/pallas_call | solution.py:291
  47.9 1.7 %copy.6 = f32[64,1024]{1,0:T(8,128)} copy(f32[64,1024]{1,0:T(8,128)} %scores.1) | data formatting | bytes 524288

commit v6 on v5

--- a/solution.py
+++ b/solution.py
@@ -259,7 +259,7 @@
 
     def finish(n):
         s2[n].wait_recv()
-        fin[n] = pk[c, n] + pk_recv[n]
+        fin[n] = (pk[c, n] + pk_recv[n]).astype(BF16)
         for dx in turn:
             if turn[n] or dx:
                 gx = lax.rem(x + dx, 4)
@@ -277,7 +277,7 @@
     for cp in os:
         cp.wait_recv()
     for n in range(8):
-        first, second = fin_recv[n // 2, 2 * (n % 2)], fin_recv[n // 2, 2 * (n % 2) + 1]
+        first, second = fin_recv[n // 2, 2 * (n % 2)].astype(F32), fin_recv[n // 2, 2 * (n % 2) + 1].astype(F32)
         out_ref[:32, n * 128:(n + 1) * 128] = jnp.where(low, first, pltpu.roll(second, 64, 1))
         out_ref[32:, n * 128:(n + 1) * 128] = jnp.where(low, pltpu.roll(first, 64, 1), second)
 
@@ -310,8 +310,8 @@
             pltpu.VMEM((4, 256, 128), F32),
             pltpu.VMEM((2, 4, 4, 32, 128), F32),
             pltpu.VMEM((4, 4, 32, 128), F32),
-            pltpu.VMEM((4, 4, 32, 128), F32),
-            pltpu.VMEM((4, 4, 32, 128), F32),
+            pltpu.VMEM((4, 4, 32, 128), BF16),
+            pltpu.VMEM((4, 4, 32, 128), BF16),
             dma((3,)), dma((2,)), dma((2,)), dma((2,)), dma((2, 20)), dma((2, 20)),
             dma((2, 2)), dma((2, 2)), dma((2,)), dma((2,)), dma((2, 2)), dma((2, 2)), dma((2, 4)), dma((2, 4)),
             dma((4,)), dma((4,)), dma((4, 4)), dma((4, 4)), pltpu.SemaphoreType.REGULAR((2,)),

time: 49.8 us -> 49.3 us (0.990)
  Pallas kernels: 47.9 us -> 47.3 us
    pallas_call x1, Pallas kernels: 47.9 us -> 47.3 us  [body(): pl.pallas_call(kernel, name='scores', out_shape=jax.ShapeDtypeStruct((64,...]
where the time goes in v6:
time: 49.3 us; the launch traced here: 49 us
  Pallas kernels  47.3 us (96%)
  local copies, waits for them, and re-layouts  1.67 us (3%)
    pallas_call x1, Pallas kernels, body(): pl.pallas_call(kernel, name='scores', out_shape=jax.ShapeDtypeStruct((64,...  47.3 us
    unnamed x1, local copies, waits for them, and re-layouts  1.67 us

profile of v6, /device:TPU:1, one launch (start us, length us, event | category | flops | bytes accessed | tf_op | source)
XLA Modules:
  0.0 49.0 jit_solution(16931517486039433324)
XLA Ops:
  0.0 47.3 %scores.1 = f32[64,1024]{1,0:T(8,128)} custom-call(bf16[2048,128]{1,0:T(8,128)(2,1)} %rows_hbm.1, s32[1,32]{1,0:T(1,128)} %lens_hbm.1, s32[1,32]{1,0:T(1,128)} %owner_hbm.1, bf16[64,4096]{1,0:T(8,128)(2,1)} %q_hbm.1), custom_call_target="tpu_custom_call" | custom-call | tf_op jit(solution)/shard_map/scores/pallas_call | solution.py:291
  47.3 1.7 %copy.6 = f32[64,1024]{1,0:T(8,128)} copy(f32[64,1024]{1,0:T(8,128)} %scores.1) | data formatting | bytes 524288

commit v7 on v6

--- a/solution.py
+++ b/solution.py
@@ -274,12 +274,15 @@
     finish(2)
     finish(3)
     fin_recv[y, x] = fin[3, x]
-    for cp in os:
-        cp.wait_recv()
-    for n in range(8):
-        first, second = fin_recv[n // 2, 2 * (n % 2)].astype(F32), fin_recv[n // 2, 2 * (n % 2) + 1].astype(F32)
-        out_ref[:32, n * 128:(n + 1) * 128] = jnp.where(low, first, pltpu.roll(second, 64, 1))
-        out_ref[32:, n * 128:(n + 1) * 128] = jnp.where(low, pltpu.roll(first, 64, 1), second)
+    for n in (3, 1, 2, 0):
+        for cp in os[4 * n:4 * n + 4]:
+            cp.wait_recv()
+        gy = lax.rem(y + 4 - turn[n], 4)
+        for m in range(2):
+            left, right = fin_recv[gy, 2 * m].astype(F32), fin_recv[gy, 2 * m + 1].astype(F32)
+            cols = pl.ds(pl.multiple_of(gy * 256 + m * 128, 128), 128)
+            out_ref[:32, cols] = jnp.where(low, left, pltpu.roll(right, 64, 1))
+            out_ref[32:, cols] = jnp.where(low, pltpu.roll(left, 64, 1), right)
 
     for cp in [*sib, *pi[0], *pi[1], *started, *swaps, *threes, *ones, *late, *s2, *os]:
         cp.wait_send()

time: 49.3 us -> 49.6 us (level)
  no operation moved by 1% of the time
where the time goes in v7:
time: 49.6 us; the launch traced here: 49.1 us
  Pallas kernels  47.4 us (96%)
  local copies, waits for them, and re-layouts  1.67 us (3%)
    pallas_call x1, Pallas kernels, body(): pl.pallas_call(kernel, name='scores', out_shape=jax.ShapeDtypeStruct((64,...  47.4 us
    unnamed x1, local copies, waits for them, and re-layouts  1.67 us

profile of v7, /device:TPU:1, one launch (start us, length us, event | category | flops | bytes accessed | tf_op | source)
XLA Modules:
  0.0 49.1 jit_solution(395060580777096500)
XLA Ops:
  0.0 47.4 %scores.1 = f32[64,1024]{1,0:T(8,128)} custom-call(bf16[2048,128]{1,0:T(8,128)(2,1)} %rows_hbm.1, s32[1,32]{1,0:T(1,128)} %lens_hbm.1, s32[1,32]{1,0:T(1,128)} %owner_hbm.1, bf16[64,4096]{1,0:T(8,128)(2,1)} %q_hbm.1), custom_call_target="tpu_custom_call" | custom-call | tf_op jit(solution)/shard_map/scores/pallas_call | solution.py:294
  47.4 1.7 %copy.6 = f32[64,1024]{1,0:T(8,128)} copy(f32[64,1024]{1,0:T(8,128)} %scores.1) | data formatting | bytes 524288
